TPU v7x, 32 devices: a whole 2x2x4 slice. The times are simulated.
32 devices in a mesh: lat: 4 (over x, core), lon: 8 (over z, y).
Axes of the slice: x: 2, y: 2, z: 4, core: 2. Of those that a mesh axis runs over, the one named last changes fastest.
Arguments:
- spectra: bfloat16 [98304, 616], P(('lat', 'lon')), may hold values from -6 to 6
- block_target: int32 [768], P(('lat', 'lon')), may hold values from 0 to 7, as said below
- block_patch: int32 [768], P(('lat', 'lon')), may hold values from 0 to 11
- block_kernel: int32 [768], P(('lat', 'lon')), may hold values from 0 to 15
- encoder_weight: bfloat16 [616, 512], replicated, may hold values from -0.25 to 0.25
- kernels: bfloat16 [16, 128, 128], replicated, may hold values from 0.049804688 to 1
- gain: float32 [512], replicated, may hold values from 0.1 to 1.9
- conv_weight: bfloat16 [3, 3, 512, 512], replicated, may hold values from -0.09375 to 0.09375
- cotangent: bfloat16 [96, 512, 512], P('lat', 'lon'), may hold values from -6 to 6
Outputs:
- conv_out: bfloat16 [96, 512, 512], P('lat', 'lon')
- conv_grad: float32 [3, 3, 512, 512], replicated
- encoder_grad: float32 [616, 512], replicated
- gain_grad: float32 [512], replicated
Inputs may be any that keep to these rules, and one draw needn't show every extreme that they name: `block_target`: within one device's 24 blocks no tile is named more than 3 times; in every latitude band one tile is named exactly 3 times by every device of the band.
All inputs are finite; a program needn't handle non-finite values.
Results may differ from a plain program's by a relative error of at most 0.0059.
Values may be sent and summed in bfloat16 or wider, within the bound.
No kernel may reach another device: no remote copies, remote signals or barrier semaphores. Data moves between devices by JAX's collectives and lax.ppermute only.
A program may use at most 192 MiB of HBM per device.

v0:
```python
import math
import jax
import jax.numpy as jnp
from jax import lax
from jax.sharding import PartitionSpec as P

PH = 8
PW = 16
MOST = 3


def padded_2(shard, sides, width, wrap):
    for axis, dim in sides:
        size, length = (lax.axis_size(axis), shard.shape[dim])
        up = [(i, (i + 1) % size) for i in range(size if wrap else size - 1)]
        down = [(j, i) for i, j in up]
        last = lax.slice_in_dim(shard, length - width, length, axis=dim)
        leading = lax.slice_in_dim(shard, 0, width, axis=dim)
        before = lax.ppermute(last, axis, up)
        after = lax.ppermute(leading, axis, down)
        shard = jnp.concatenate([before, shard, after], axis=dim)
    return shard


def normalise(field, gain):
    meansq = jnp.mean(field * field, axis=-1, keepdims=True)
    return field * lax.rsqrt(meansq + 1e-06) * gain


def silu_slope(preact):
    logistic = jax.nn.sigmoid(preact)
    return logistic * (1.0 + preact * (1.0 - logistic))


def widen(field):
    beside_all = padded_2(field, (("lon", 1),), 1, True)
    return padded_2(beside_all, (("lat", 0),), 1, False)


def slot_layout(targets, lon_count):
    lanes = jnp.arange(lon_count, dtype=jnp.int32)
    onehot = (targets[..., None] == lanes).astype(jnp.int32)
    before = jnp.cumsum(onehot, axis=-2) - onehot
    ranks = jnp.sum(before * onehot, axis=-1)
    return targets * MOST + ranks


def to_tile(patches_in, tile_rows, tile_cols, width):
    shaped = patches_in.reshape(tile_rows // PH, tile_cols // PW, PH, PW, width)
    return shaped.transpose(0, 2, 1, 3, 4).reshape(tile_rows, tile_cols, width)


def to_patches(tile, tile_rows, tile_cols, width):
    shaped = tile.reshape(tile_rows // PH, PH, tile_cols // PW, PW, width)
    return shaped.transpose(0, 2, 1, 3, 4).reshape(-1, PH * PW, width)


def shards(
    spectra,
    block_target,
    block_patch,
    block_kernel,
    encoder_weight,
    kernels,
    gain,
    conv_weight,
    cotangent,
):
    lon_count = lax.axis_size("lon")
    lat_count = lax.axis_size("lat")
    own_lon = lax.axis_index("lon")
    blocks = block_target.shape[0]
    kernel_count, block_rows, patch_cells = kernels.shape
    channels = spectra.shape[1]
    width = encoder_weight.shape[1]
    tile_rows, tile_cols = (cotangent.shape[0], cotangent.shape[1])
    slots = lon_count * MOST
    patch_count = tile_rows // PH * (tile_cols // PW)
    loss_scale = 1.0 / math.sqrt(tile_rows * lat_count * tile_cols * lon_count)
    all_target, all_patch, all_kernel = (
        lax.all_gather(block_target, "lon", axis=0, tiled=True),
        lax.all_gather(block_patch, "lon", axis=0, tiled=True),
        lax.all_gather(block_kernel, "lon", axis=0, tiled=True),
    )
    all_target = all_target.reshape(lon_count, blocks)
    all_patch = all_patch.reshape(lon_count, blocks)
    all_kernel = all_kernel.reshape(lon_count, blocks)
    own_slot = slot_layout(block_target, lon_count)
    slot_ids = jnp.arange(slots, dtype=jnp.int32)
    chosen_slots = own_slot[None, :] == slot_ids[:, None]
    filled = jnp.any(chosen_slots, axis=1)
    source_block = jnp.sum(chosen_slots * jnp.arange(blocks, dtype=jnp.int32)[None, :], axis=1)
    all_slot = slot_layout(all_target, lon_count)
    wanted = own_lon * MOST + jnp.arange(MOST, dtype=jnp.int32)
    arrive = (all_slot[:, None, :] == wanted[None, :, None]).astype(jnp.int32)
    present = jnp.sum(arrive, axis=2).reshape(-1) > 0
    slot_kernel = jnp.sum(arrive * all_kernel[:, None, :], axis=2).reshape(-1)
    slot_kernel = jnp.where(present, slot_kernel, -1)
    slot_patch = jnp.sum(arrive * all_patch[:, None, :], axis=2).reshape(-1)
    taken = jnp.take(spectra.reshape(blocks, block_rows, channels), source_block, axis=0)
    taken = jnp.where(filled[:, None, None], taken, jnp.zeros_like(taken))
    arrived = lax.all_to_all(
        taken.reshape(lon_count, MOST, -1), "lon", split_axis=0, concat_axis=0, tiled=True
    )
    slot_spectra = arrived.reshape(slots * block_rows, channels)
    slot_preact = jnp.dot(slot_spectra, encoder_weight, preferred_element_type=jnp.float32)
    slot_rows = jax.nn.silu(slot_preact).astype(jnp.bfloat16).reshape(slots, block_rows, width)
    kernel_pick = (
        slot_kernel[:, None] == jnp.arange(kernel_count, dtype=jnp.int32)[None, :]
    ).astype(jnp.bfloat16)
    slot_kernels = jnp.dot(
        kernel_pick, kernels.reshape(kernel_count, -1), preferred_element_type=jnp.float32
    )
    slot_kernels = slot_kernels.astype(jnp.bfloat16).reshape(slots, block_rows, patch_cells)
    contribution = jnp.einsum(
        "sbp,sbd->spd", slot_kernels, slot_rows, preferred_element_type=jnp.float32
    )
    patch_pick = (slot_patch[:, None] == jnp.arange(patch_count, dtype=jnp.int32)[None, :]).astype(
        jnp.float32
    )
    tile_patches = jnp.einsum(
        "sq,spd->qpd", patch_pick, contribution, precision=lax.Precision.HIGHEST
    )
    spread = to_tile(tile_patches, tile_rows, tile_cols, width)
    normed = normalise(spread, gain).astype(jnp.bfloat16)
    padded = widen(normed)
    windows = []
    result_sum = jnp.zeros((tile_rows * tile_cols, width), jnp.float32)
    for row_shift in range(3):
        for col_shift in range(3):
            window = padded[
                row_shift : row_shift + tile_rows, col_shift : col_shift + tile_cols
            ].reshape(-1, width)
            windows.append(window)
            result_sum = result_sum + jnp.dot(
                window, conv_weight[row_shift, col_shift], preferred_element_type=jnp.float32
            )
    conv_out = result_sum.reshape(tile_rows, tile_cols, width).astype(jnp.bfloat16)
    cot_padded = widen(cotangent)
    cot_flat = cotangent.reshape(-1, width)
    d_normed = jnp.zeros((tile_rows * tile_cols, width), jnp.float32)
    kernel_grads = []
    for row_shift in range(3):
        for col_shift in range(3):
            back_window = cot_padded[
                2 - row_shift : 2 - row_shift + tile_rows, 2 - col_shift : 2 - col_shift + tile_cols
            ].reshape(-1, width)
            d_normed = d_normed + lax.dot_general(
                back_window,
                conv_weight[row_shift, col_shift],
                (((1,), (1,)), ((), ())),
                preferred_element_type=jnp.float32,
            )
            kernel_grads.append(
                lax.dot_general(
                    windows[row_shift * 3 + col_shift],
                    cot_flat,
                    (((0,), (0,)), ((), ())),
                    preferred_element_type=jnp.float32,
                )
            )
    conv_part = jnp.stack(kernel_grads).reshape(3, 3, width, width)
    _, pullback = jax.vjp(normalise, spread, gain)
    d_spread, gain_part = pullback(d_normed.reshape(tile_rows, tile_cols, width))
    d_patches = to_patches(d_spread.astype(jnp.bfloat16), tile_rows, tile_cols, width)
    slot_dpatch = jnp.take(d_patches, slot_patch, axis=0)
    slot_drows = jnp.einsum(
        "sbp,spd->sbd", slot_kernels, slot_dpatch, preferred_element_type=jnp.float32
    ).astype(jnp.bfloat16)
    d_preact = (slot_drows.reshape(-1, width).astype(jnp.float32) * silu_slope(slot_preact)).astype(
        jnp.bfloat16
    )
    encoder_part = lax.dot_general(
        slot_spectra, d_preact, (((0,), (0,)), ((), ())), preferred_element_type=jnp.float32
    )
    conv_total, encoder_total, gain_total = lax.psum(
        (conv_part, encoder_part, gain_part), ("lat", "lon")
    )
    return (conv_out, conv_total * loss_scale, encoder_total * loss_scale, gain_total * loss_scale)


def solution(mesh):
    placed = (
        P(("lat", "lon"), None),
        P(("lat", "lon")),
        P(("lat", "lon")),
        P(("lat", "lon")),
        P(),
        P(),
        P(),
        P(),
        P("lat", "lon", None),
    )
    return jax.shard_map(
        shards,
        mesh=mesh,
        in_specs=placed,
        out_specs=(P("lat", "lon", None), P(), P(), P()),
        check_vma=False,
    )
```

profile of v0, /device:TPU:0, one launch (start us, length us, event | category | flops | bytes accessed | tf_op | source)
XLA Modules:
  0.0 510.4 jit_solution(6960326215886359969)
XLA Ops:
  9.8 1.2 dynamic-slice
  14.3 13.1 %all-reduce.3 = (s32[192]{0:T(256)S(1)}, s32[192]{0:T(256)S(1)}, s32[192]{0:T(256)S(1)}) all-reduce(s32[192]{0:T(256)S(1)} %dynamic-update-slice.1, s32[192]{0:T(256)S(1)} %dynamic-update-slice, s32[192]{0:T(256)S(1)} %dynamic-update-slice.2), channel_id=1, replica_groups=mesh['lat'=4,'lon'=8] {'lon'}, use_global_device_ids=true, to_apply=%add.1 | all-reduce | flops 576 | bytes 4608
  29.1 4.6 copy_bitcast_fusion
  33.7 5.1 gather_fusion
  38.8 6.2 %copy.96 = bf16[24,128,616]{2,1,0:T(8,128)(2,1)} copy(bf16[24,128,616]{1,2,0:T(8,128)(2,1)} %gather_fusion) | data formatting | bytes 7569408 | tf_op jit(solution)/shard_map/jit(_take)/gather | solution.py:100
  45.1 10.8 %gather.11 = bf16[8,3,78848]{2,1,0:T(4,128)(2,1)} reshape(bf16[24,128,616]{2,1,0:T(8,128)(2,1)} %copy.96) | data formatting | bytes 7569408 | tf_op jit(solution)/shard_map/jit(_take)/gather | solution.py:100
  55.9 7.2 %select_select_fusion = bf16[8,3,78848]{2,1,0:T(4,128)(2,1)} fusion(bf16[8,3,78848]{2,1,0:T(4,128)(2,1)} %gather.11, pred[8,3]{1,0:T(8,128)(4,1)S(1)} %copy.94, pred[8,3]{1,0:T(8,128)(4,1)S(1)} %broadcast_in_dim.57), kind=kLoop, calls=%fused_computation.9 | loop fusion | flops 3784704 | bytes 7569456 | tf_op jit(solution)/shard_map/jit(_where)/select_n | solution.py:101
  63.1 4.8 all-to-all-start
  68.0 1.9 collective-permute-start.4
  69.9 2.9 collective-permute-start.5
  73.0 2.1 fusion.41
  75.8 76.7 %collective-permute-done.4 = bf16[24,1,512]{2,1,0:T(2,128)(2,1)S(1)} collective-permute-done((bf16[24,1,512]{2,1,0:T(2,128)(2,1)S(1)}, bf16[24,1,512]{2,1,0:T(2,128)(2,1)S(1)}, u32[]{:S(2)}, u32[]{:S(2)}) %collective-permute-start.4) | collective-permute-done | bytes 24608 | tf_op jit(solution)/shard_map/ppermute | solution.py:19
  152.6 1.3 collective-permute-start.6
  153.9 3.2 collective-permute-start.7
  157.1 1.1 pad_maximum_fusion.2
  158.2 2.0 pad_maximum_fusion.1
  160.3 2.3 fusion.96
  163.7 1.0 fusion.49
  164.7 1.1 convolution_add_fusion.5
  165.8 1.0 convolution_add_fusion.4
  166.9 1.1 fusion.4
  168.0 1.1 fusion.3
  169.1 1.0 convolution_add_fusion.1
  170.1 2.7 convolution_add_fusion
  172.8 4.4 all-to-all-done
  177.2 10.9 %reshape.259 = bf16[3072,616]{1,0:T(8,128)(2,1)} reshape(bf16[8,3,78848]{2,1,0:T(4,128)(2,1)} %all-to-all-done) | data formatting | bytes 7569408 | tf_op jit(solution)/shard_map/reshape | solution.py:105
  188.0 7.0 %multiply_convert_fusion = (bf16[3072,512]{1,0:T(8,128)(2,1)S(1)}, f32[3072,512]{1,0:T(8,128)}) fusion(bf16[3072,616]{1,0:T(8,128)(2,1)} %reshape.259, bf16[616,512]{1,0:T(8,128)(2,1)S(1)} %copy-done), kind=kOutput, calls=%fused_computation.7 | convolution fusion | flops 1945632768 | bytes 13852672 | tf_op jit(solution)/shard_map/dot_general | solution.py:106
  195.0 1.0 fusion.101
  196.1 6.3 %fusion.1 = f32[12,128,512]{2,0,1:T(8,128)S(1)} fusion(f32[24,128,512]{2,1,0:T(8,128)S(1)} %fusion.101, s32[24]{0:T(128)S(1)} %eq.86), kind=kOutput, calls=%fused_computation.5 | convolution fusion | flops 226492704 | bytes 9437280 | tf_op jit(solution)/shard_map/sq,spd->qpd/dot_general | solution.py:121
  202.4 1.8 copy.99
  204.2 2.0 copy.100
  206.2 1.1 copy-done.3
  209.1 4.7 fusion.7
  214.2 1.1 copy-done.6
  215.4 2.1 collective-permute-start
  217.5 2.9 collective-permute-start.1
  220.3 3.9 gather_fusion.1
  224.3 2.9 fusion.14
  227.2 4.5 fusion
  231.7 3.2 fusion.102
  234.9 1.3 collective-permute-start.2
  236.2 1.3 collective-permute-start.3
  237.5 1.1 pad_maximum_fusion.4
  238.7 2.4 collective-permute-done.3
  241.1 2.0 maximum_maximum_fusion
  244.2 1.0 fusion.25
  245.2 1.0 fusion.24
  249.3 1.0 fusion.20
  250.3 1.0 fusion.19
  251.4 1.0 fusion.18
  252.4 3.7 copy-done.18
  256.3 1.3 copy-done.19
  257.6 1.3 copy.102
  258.9 2.3 fusion.9
  261.2 61.9 %psum.23 = f32[512]{0:T(512)S(1)} all-reduce(f32[512]{0:T(512)S(1)} %fusion.9), channel_id=1, replica_groups=mesh['lat'=4,'lon'=8] {'lat','lon'}, use_global_device_ids=true, to_apply=%region_14.15 | all-reduce | flops 512 | bytes 4096 | tf_op jit(solution)/shard_map/psum | solution.py:176
  323.7 2.7 fusion.43
  326.4 1.1 fusion.95
  329.2 1.1 fusion.94
  331.2 1.0 convolution_add_fusion.11
  332.3 1.1 convolution_add_fusion.10
  337.1 2.1 fusion.13
  339.2 153.7 %all-reduce.7.cloned.1.call-done = (f32[3,3,512,512]{3,2,1,0:T(8,128)}, f32[616,512]{1,0:T(8,128)}) async-done(((f32[3,3,512,512]{3,2,1,0:T(8,128)}, f32[616,512]{1,0:T(8,128)}), (f32[3,3,512,512]{3,2,1,0:T(8,128)}, f32[616,512]{1,0:T(8,128)})) %all-reduce.7.cloned.1.call-update) | async-done | bytes 10698768 | tf_op jit(solution)/shard_map/psum | solution.py:176
  492.9 9.2 %broadcast_multiply_fusion = f32[3,3,512,512]{3,2,1,0:T(8,128)} fusion(f32[3,3,512,512]{3,2,1,0:T(8,128)} %get-tuple-element.12), kind=kLoop, calls=%fused_computation.11 | loop fusion | flops 2359296 | bytes 18874368 | tf_op jit(solution)/shard_map/mul | solution.py:179
  502.1 1.2 broadcast_multiply_fusion.1
  (119 shorter events, 22.4 us)
Async XLA Ops:
  7.2 180.9 %copy-start = (bf16[616,512]{1,0:T(8,128)(2,1)S(1)}, bf16[616,512]{1,0:T(8,128)(2,1)}, u32[]{:S(2)}) copy-start(bf16[616,512]{1,0:T(8,128)(2,1)} %param.13) | copy-start | bytes 1892356
  63.1 4.8 copy-start.2
  63.1 114.1 %all-to-all-start = ((bf16[8,3,78848]{2,1,0:T(4,128)(2,1)}), bf16[8,3,78848]{2,1,0:T(4,128)(2,1)}, u32[]{:S(2)}, u32[]{:S(2)}) async-start(bf16[8,3,78848]{2,1,0:T(4,128)(2,1)} %select_select_fusion), calls=%async_computation | async-start | bytes 10092544 | tf_op jit(solution)/shard_map/all_to_all | solution.py:102
  67.8 425.1 %all-reduce.7.cloned.1.call-start = ((), (), s32[]{:S(2)}) async-start(), calls=%async_computation.1 | async-start | bytes 21397504 | tf_op jit(solution)/shard_map/psum | solution.py:176
  68.0 84.6 %collective-permute-start.4 = (bf16[24,1,512]{2,1,0:T(2,128)(2,1)S(1)}, bf16[24,1,512]{2,1,0:T(2,128)(2,1)S(1)}, u32[]{:S(2)}, u32[]{:S(2)}) collective-permute-start(bf16[24,1,512]{2,1,0:T(2,128)(2,1)S(1)} %get-tuple-element.42), channel_id=1, source_target_pairs={{0,1},{1,2},{2,3},{3,4},{4,5},{5,6},{6,7},{7,0},{8,9},{9,10},{10,1... | collective-permute-start | bytes 73736 | tf_op jit(solution)/shard_map/ppermute | solution.py:19
  69.9 82.7 %collective-permute-start.5 = (bf16[24,1,512]{2,1,0:T(2,128)(2,1)S(1)}, bf16[24,1,512]{2,1,0:T(2,128)(2,1)S(1)}, u32[]{:S(2)}, u32[]{:S(2)}) collective-permute-start(bf16[24,1,512]{2,1,0:T(2,128)(2,1)S(1)} %get-tuple-element.43), channel_id=1, source_target_pairs={{1,0},{2,1},{3,2},{4,3},{5,4},{6,5},{7,6},{0,7},{9,8},{10,9},{11,1... | collective-permute-start | bytes 73736 | tf_op jit(solution)/shard_map/ppermute | solution.py:20
  73.0 2.2 copy-start.21
  152.6 5.6 %collective-permute-start.6 = (bf16[1,66,512]{2,1,0:T(8,128)(2,1)S(1)}, bf16[1,66,512]{2,1,0:T(8,128)(2,1)S(1)}, u32[]{:S(2)}, u32[]{:S(2)}) collective-permute-start(bf16[1,66,512]{2,1,0:T(8,128)(2,1)S(1)} %get-tuple-element.34), channel_id=1, source_target_pairs={{8,0},{16,8},{24,16},{9,1},{17,9},{25,17},{10,2},{18,10},{26,18},{... | collective-permute-start | bytes 202760 | tf_op jit(solution)/shard_map/ppermute | solution.py:20
  153.9 4.3 collective-permute-start.7
  158.2 4.4 slice-start
  160.3 2.4 slice-start.1
  204.2 3.2 copy-start.3
  204.2 4.2 copy-start.4
  204.2 4.2 copy-start.22
  209.1 4.7 copy-start.11
  214.2 1.1 copy-start.6
  215.4 19.5 %collective-permute-start = (bf16[24,1,512]{2,1,0:T(2,128)(2,1)S(1)}, bf16[24,1,512]{2,1,0:T(2,128)(2,1)S(1)}, u32[]{:S(2)}, u32[]{:S(2)}) collective-permute-start(bf16[24,1,512]{2,1,0:T(2,128)(2,1)S(1)} %get-tuple-element.38), channel_id=1, source_target_pairs={{0,1},{1,2},{2,3},{3,4},{4,5},{5,6},{6,7},{7,0},{8,9},{9,10},{10,1... | collective-permute-start | bytes 73736 | tf_op jit(solution)/shard_map/ppermute | solution.py:19
  217.5 17.4 %collective-permute-start.1 = (bf16[24,1,512]{2,1,0:T(2,128)(2,1)S(1)}, bf16[24,1,512]{2,1,0:T(2,128)(2,1)S(1)}, u32[]{:S(2)}, u32[]{:S(2)}) collective-permute-start(bf16[24,1,512]{2,1,0:T(2,128)(2,1)S(1)} %get-tuple-element.39), channel_id=1, source_target_pairs={{1,0},{2,1},{3,2},{4,3},{5,4},{6,5},{7,6},{0,7},{9,8},{10,9},{11,1... | collective-permute-start | bytes 73736 | tf_op jit(solution)/shard_map/ppermute | solution.py:20
  227.2 4.5 copy-start.10
  231.7 3.2 copy-start.7
  234.9 3.7 collective-permute-start.2
  236.2 4.9 collective-permute-start.3
  238.7 7.6 %copy-start.16 = (bf16[24,64,512]{2,1,0:T(8,128)(2,1)}, bf16[24,64,512]{2,1,0:T(8,128)(2,1)S(1)}, u32[]{:S(2)}) copy-start(bf16[24,64,512]{2,1,0:T(8,128)(2,1)S(1)} %get-tuple-element.37) | copy-start | bytes 4718596
  238.7 9.6 %copy-start.14 = (bf16[24,64,512]{2,1,0:T(8,128)(2,1)}, bf16[24,64,512]{2,1,0:T(8,128)(2,1)S(1)}, u32[]{:S(2)}) copy-start(bf16[24,64,512]{2,1,0:T(8,128)(2,1)S(1)} %get-tuple-element.36) | copy-start | bytes 4718596
  243.2 2.1 copy-start.12
  243.2 8.2 %copy-start.8 = (bf16[25,66,512]{2,1,0:T(8,128)(2,1)}, bf16[25,66,512]{2,1,0:T(8,128)(2,1)S(1)}, u32[]{:S(2)}) copy-start(bf16[25,66,512]{2,1,0:T(8,128)(2,1)S(1)} %get-tuple-element.29) | copy-start | bytes 5068804
  252.4 3.7 copy-start.18
  256.2 1.4 copy-start.19
  256.3 2.6 copy-start.5
  323.7 2.7 copy-start.13
  323.7 3.8 slice-start.2
  326.4 1.3 slice-start.3
  327.6 1.5 copy-start.9
  332.3 1.4 copy-start.17
  333.7 1.4 copy-start.15
  492.9 9.2 %copy-start.20 = (f32[616,512]{1,0:T(8,128)S(1)}, f32[616,512]{1,0:T(8,128)}, u32[]{:S(2)}) copy-start(f32[616,512]{1,0:T(8,128)} %get-tuple-element.13) | copy-start | bytes 3784708
  492.9 10.4 %copy-start.1 = (bf16[616,512]{1,0:T(8,128)(2,1)S(1)}, bf16[616,512]{1,0:T(8,128)(2,1)}, u32[]{:S(2)}) copy-start(bf16[616,512]{1,0:T(8,128)(2,1)} %param.13) | copy-start | bytes 1892356
Sparse Core Ops, SparseCore 0:
  256.3 236.5 all-reduce.6
where the time goes:
time: 518 us; the launch traced here: 510 us
  waiting for transfers between devices  237 us (46%)
  blocking collectives  75 us (14%)
  local copies, waits for them, and re-layouts  66.4 us (13%)
  matrix products  54.1 us (10%)
  other arithmetic  40.5 us (8%)
  starting transfers between devices  21.6 us (4%)
  between operations  15.6 us (3%)
    psum x1, waiting for transfers between devices, shards(): lax.psum((conv_part, encoder_part, gain_part), ('lat', 'lon'))  154 us
    ppermute x4, waiting for transfers between devices, padded_2(): before = lax.ppermute(last, axis, up)  76.7 us
    psum x1, blocking collectives, shards(): lax.psum((conv_part, encoder_part, gain_part), ('lat', 'lon'))  61.9 us
    gather x3, local copies, waits for them, and re-layouts, shards(): jnp.take(spectra.reshape(blocks, block_rows, channels), source_block, axi...  22.1 us
    unnamed x62, local copies, waits for them, and re-layouts  13.8 us
    unnamed x1, blocking collectives  13.1 us
    dot_general x9, matrix products, shards(): lax.dot_general(back_window, conv_weight[row_shift, col_shift], (((1,), (...  12.2 us
    dot_general x9, matrix products, shards(): jnp.dot(window, conv_weight[row_shift, col_shift], preferred_element_type...  11.8 us
  transfers between devices with their start and end apart: 10, of which 4 were waited for; matrix products, arithmetic and copies ran while one was open for 10% of the time, Pallas kernels for 0%

commit v1 on v0

--- a/solution.py
+++ b/solution.py
@@ -174,7 +174,7 @@
         slot_spectra, d_preact, (((0,), (0,)), ((), ())), preferred_element_type=jnp.float32
     )
     conv_total, encoder_total, gain_total = lax.psum(
-        (conv_part, encoder_part, gain_part), ("lat", "lon")
+        lax.psum((conv_part, encoder_part, gain_part), "lon"), "lat"
     )
     return (conv_out, conv_total * loss_scale, encoder_total * loss_scale, gain_total * loss_scale)
 

time: 518 us -> 828 us (1.60)
  waiting for transfers between devices: 237 us -> 583 us
  blocking collectives: 75 us -> 39 us
    psum x1 -> x2, waiting for transfers between devices: 154 us -> 500 us  [the longest x1 354 us: shards(): lax.psum((conv_part, encoder_part, gain_part), 'lon')]
    psum x1 -> x2, blocking collectives: 61.9 us -> 25.9 us  [the longest x1 19.2 us: shards(): lax.psum((conv_part, encoder_part, gain_part), 'lon')]
  transfers between devices with their start and end apart: 10 -> 11, of which waited for: 4 -> 5; matrix products, arithmetic and copies ran while one was open for 10% -> 6% of each run, Pallas kernels for 0% -> 0%
where the time goes in v1:
time: 828 us; the launch traced here: 820 us
  waiting for transfers between devices  583 us (70%)
  local copies, waits for them, and re-layouts  65.9 us (8%)
  matrix products  53.6 us (6%)
  other arithmetic  40.5 us (5%)
  blocking collectives  39 us (5%)
  starting transfers between devices  21.6 us (3%)
  between operations  15.6 us (2%)
    psum x1, waiting for transfers between devices, shards(): lax.psum((conv_part, encoder_part, gain_part), 'lon')  354 us
    psum x1, waiting for transfers between devices, shards(): lax.psum(lax.psum((conv_part, encoder_part, gain_part), 'lon'), 'lat')  146 us
    ppermute x4, waiting for transfers between devices, padded_2(): before = lax.ppermute(last, axis, up)  76.7 us
    gather x3, local copies, waits for them, and re-layouts, shards(): jnp.take(spectra.reshape(blocks, block_rows, channels), source_block, axi...  22 us
    psum x1, blocking collectives, shards(): lax.psum((conv_part, encoder_part, gain_part), 'lon')  19.2 us
  transfers between devices with their start and end apart: 11, of which 5 were waited for; matrix products, arithmetic and copies ran while one was open for 6% of the time, Pallas kernels for 0%

profile of v1, /device:TPU:0, one launch (start us, length us, event | category | flops | bytes accessed | tf_op | source)
XLA Modules:
  0.0 819.6 jit_solution(14661528217365656713)
XLA Ops:
  9.8 1.2 dynamic-slice
  14.3 13.1 %all-reduce.3 = (s32[192]{0:T(256)S(1)}, s32[192]{0:T(256)S(1)}, s32[192]{0:T(256)S(1)}) all-reduce(s32[192]{0:T(256)S(1)} %dynamic-update-slice.1, s32[192]{0:T(256)S(1)} %dynamic-update-slice, s32[192]{0:T(256)S(1)} %dynamic-update-slice.2), channel_id=1, replica_groups=mesh['lat'=4,'lon'=8] {'lon'}, use_global_device_ids=true, to_apply=%add.1 | all-reduce | flops 576 | bytes 4608
  29.1 4.6 copy_bitcast_fusion
  33.7 5.1 gather_fusion
  38.8 6.1 copy.96
  45.0 10.8 %gather.11 = bf16[8,3,78848]{2,1,0:T(4,128)(2,1)} reshape(bf16[24,128,616]{2,1,0:T(8,128)(2,1)} %copy.96) | data formatting | bytes 7569408 | tf_op jit(solution)/shard_map/jit(_take)/gather | solution.py:100
  55.7 7.2 select_select_fusion
  62.9 4.8 all-to-all-start
  67.9 1.9 collective-permute-start.4
  69.8 2.9 collective-permute-start.5
  72.9 2.1 fusion.41
  75.7 76.7 %collective-permute-done.4 = bf16[24,1,512]{2,1,0:T(2,128)(2,1)S(1)} collective-permute-done((bf16[24,1,512]{2,1,0:T(2,128)(2,1)S(1)}, bf16[24,1,512]{2,1,0:T(2,128)(2,1)S(1)}, u32[]{:S(2)}, u32[]{:S(2)}) %collective-permute-start.4) | collective-permute-done | bytes 24608 | tf_op jit(solution)/shard_map/ppermute | solution.py:19
  152.5 1.3 collective-permute-start.6
  153.8 3.2 collective-permute-start.7
  157.0 1.1 pad_maximum_fusion.2
  158.1 2.0 pad_maximum_fusion.1
  160.2 2.3 fusion.96
  163.6 1.0 fusion.49
  164.6 1.1 convolution_add_fusion.5
  165.7 1.0 convolution_add_fusion.4
  166.7 1.1 fusion.4
  167.8 1.1 fusion.3
  168.9 1.0 convolution_add_fusion.1
  170.0 2.7 convolution_add_fusion
  172.7 4.4 all-to-all-done
  177.1 10.8 %reshape.259 = bf16[3072,616]{1,0:T(8,128)(2,1)} reshape(bf16[8,3,78848]{2,1,0:T(4,128)(2,1)} %all-to-all-done) | data formatting | bytes 7569408 | tf_op jit(solution)/shard_map/reshape | solution.py:105
  187.9 7.0 multiply_convert_fusion
  195.9 6.3 fusion.1
  202.2 1.8 copy.99
  204.1 2.0 copy.100
  206.1 1.1 copy-done.3
  209.0 4.7 fusion.7
  214.0 1.1 copy-done.6
  215.3 2.0 collective-permute-start
  217.3 2.9 collective-permute-start.1
  220.2 3.9 gather_fusion.1
  224.1 2.9 fusion.14
  227.1 4.5 fusion
  231.5 3.2 fusion.102
  234.8 1.3 collective-permute-start.2
  236.1 1.3 collective-permute-start.3
  237.4 1.1 pad_maximum_fusion.4
  238.5 2.4 collective-permute-done.3
  241.0 2.0 maximum_maximum_fusion
  244.1 1.0 fusion.25
  245.1 1.0 fusion.24
  250.2 1.0 fusion.19
  251.2 1.0 fusion.18
  252.3 3.7 copy-done.18
  256.1 353.5 %all-reduce.9.cloned.1.call-done = (f32[3,3,512,512]{3,2,1,0:T(8,128)}, f32[616,512]{1,0:T(8,128)}) async-done(((f32[3,3,512,512]{3,2,1,0:T(8,128)}, f32[616,512]{1,0:T(8,128)}), (f32[3,3,512,512]{3,2,1,0:T(8,128)}, f32[616,512]{1,0:T(8,128)})) %all-reduce.9.cloned.1.call-update) | async-done | bytes 10698768 | tf_op jit(solution)/shard_map/psum | solution.py:177
  609.8 1.7 copy.102
  612.1 2.3 fusion.9
  614.5 19.2 %psum.46 = f32[512]{0:T(512)S(1)} all-reduce(f32[512]{0:T(512)S(1)} %fusion.9), channel_id=1, replica_groups=mesh['lat'=4,'lon'=8] {'lon'}, use_global_device_ids=true, to_apply=%region_16.17 | all-reduce | flops 512 | bytes 4096 | tf_op jit(solution)/shard_map/psum | solution.py:177
  633.7 6.7 psum.47
  640.9 2.2 fusion.43
  643.1 1.1 fusion.95
  645.9 1.1 fusion.94
  647.9 1.1 convolution_add_fusion.11
  649.0 1.1 convolution_add_fusion.10
  650.4 1.1 fusion.6
  653.8 2.1 fusion.13
  655.9 146.2 %all-reduce.11.cloned.1.call-done = (f32[3,3,512,512]{3,2,1,0:T(8,128)}, f32[616,512]{1,0:T(8,128)}) async-done(((f32[3,3,512,512]{3,2,1,0:T(8,128)}, f32[616,512]{1,0:T(8,128)}), (f32[3,3,512,512]{3,2,1,0:T(8,128)}, f32[616,512]{1,0:T(8,128)})) %all-reduce.11.cloned.1.call-update) | async-done | bytes 10698768 | tf_op jit(solution)/shard_map/psum | solution.py:176
  802.1 9.2 %broadcast_multiply_fusion = f32[3,3,512,512]{3,2,1,0:T(8,128)} fusion(f32[3,3,512,512]{3,2,1,0:T(8,128)} %get-tuple-element.14), kind=kLoop, calls=%fused_computation.11 | loop fusion | flops 2359296 | bytes 18874368 | tf_op jit(solution)/shard_map/mul | solution.py:179
  811.4 1.2 broadcast_multiply_fusion.1
  (121 shorter events, 24.0 us)
Async XLA Ops:
  7.2 180.7 %copy-start = (bf16[616,512]{1,0:T(8,128)(2,1)S(1)}, bf16[616,512]{1,0:T(8,128)(2,1)}, u32[]{:S(2)}) copy-start(bf16[616,512]{1,0:T(8,128)(2,1)} %param.13) | copy-start | bytes 1892356
  62.9 4.8 copy-start.2
  62.9 114.1 %all-to-all-start = ((bf16[8,3,78848]{2,1,0:T(4,128)(2,1)}), bf16[8,3,78848]{2,1,0:T(4,128)(2,1)}, u32[]{:S(2)}, u32[]{:S(2)}) async-start(bf16[8,3,78848]{2,1,0:T(4,128)(2,1)} %select_select_fusion), calls=%async_computation | async-start | bytes 10092544 | tf_op jit(solution)/shard_map/all_to_all | solution.py:102
  67.7 541.9 %all-reduce.9.cloned.1.call-start = ((), (), s32[]{:S(2)}) async-start(), calls=%async_computation.1 | async-start | bytes 21397504 | tf_op jit(solution)/shard_map/psum | solution.py:177
  67.9 84.6 %collective-permute-start.4 = (bf16[24,1,512]{2,1,0:T(2,128)(2,1)S(1)}, bf16[24,1,512]{2,1,0:T(2,128)(2,1)S(1)}, u32[]{:S(2)}, u32[]{:S(2)}) collective-permute-start(bf16[24,1,512]{2,1,0:T(2,128)(2,1)S(1)} %get-tuple-element.44), channel_id=1, source_target_pairs={{0,1},{1,2},{2,3},{3,4},{4,5},{5,6},{6,7},{7,0},{8,9},{9,10},{10,1... | collective-permute-start | bytes 73736 | tf_op jit(solution)/shard_map/ppermute | solution.py:19
  69.8 82.7 %collective-permute-start.5 = (bf16[24,1,512]{2,1,0:T(2,128)(2,1)S(1)}, bf16[24,1,512]{2,1,0:T(2,128)(2,1)S(1)}, u32[]{:S(2)}, u32[]{:S(2)}) collective-permute-start(bf16[24,1,512]{2,1,0:T(2,128)(2,1)S(1)} %get-tuple-element.45), channel_id=1, source_target_pairs={{1,0},{2,1},{3,2},{4,3},{5,4},{6,5},{7,6},{0,7},{9,8},{10,9},{11,1... | collective-permute-start | bytes 73736 | tf_op jit(solution)/shard_map/ppermute | solution.py:20
  72.9 2.2 copy-start.20
  152.5 5.6 collective-permute-start.6
  153.8 4.3 collective-permute-start.7
  158.1 4.4 slice-start
  160.1 2.4 slice-start.1
  204.1 3.2 copy-start.3
  204.1 4.2 copy-start.4
  204.1 4.2 copy-start.21
  209.0 4.7 copy-start.11
  214.0 1.1 copy-start.6
  215.3 19.5 %collective-permute-start = (bf16[24,1,512]{2,1,0:T(2,128)(2,1)S(1)}, bf16[24,1,512]{2,1,0:T(2,128)(2,1)S(1)}, u32[]{:S(2)}, u32[]{:S(2)}) collective-permute-start(bf16[24,1,512]{2,1,0:T(2,128)(2,1)S(1)} %get-tuple-element.40), channel_id=1, source_target_pairs={{0,1},{1,2},{2,3},{3,4},{4,5},{5,6},{6,7},{7,0},{8,9},{9,10},{10,1... | collective-permute-start | bytes 73736 | tf_op jit(solution)/shard_map/ppermute | solution.py:19
  217.3 17.4 %collective-permute-start.1 = (bf16[24,1,512]{2,1,0:T(2,128)(2,1)S(1)}, bf16[24,1,512]{2,1,0:T(2,128)(2,1)S(1)}, u32[]{:S(2)}, u32[]{:S(2)}) collective-permute-start(bf16[24,1,512]{2,1,0:T(2,128)(2,1)S(1)} %get-tuple-element.41), channel_id=1, source_target_pairs={{1,0},{2,1},{3,2},{4,3},{5,4},{6,5},{7,6},{0,7},{9,8},{10,9},{11,1... | collective-permute-start | bytes 73736 | tf_op jit(solution)/shard_map/ppermute | solution.py:20
  227.1 4.5 copy-start.10
  231.5 3.2 copy-start.7
  234.8 3.7 collective-permute-start.2
  236.1 4.9 collective-permute-start.3
  238.5 7.6 copy-start.16
  238.5 9.6 %copy-start.14 = (bf16[24,64,512]{2,1,0:T(8,128)(2,1)}, bf16[24,64,512]{2,1,0:T(8,128)(2,1)S(1)}, u32[]{:S(2)}) copy-start(bf16[24,64,512]{2,1,0:T(8,128)(2,1)S(1)} %get-tuple-element.38) | copy-start | bytes 4718596
  243.0 2.1 copy-start.12
  243.0 8.2 copy-start.8
  252.3 3.7 copy-start.18
  256.0 546.1 %all-reduce.11.cloned.1.call-start = ((), (), s32[]{:S(2)}) async-start(), calls=%async_computation.2 | async-start | bytes 21397504 | tf_op jit(solution)/shard_map/psum | solution.py:176
  609.7 2.4 copy-start.5
  640.9 2.2 copy-start.13
  640.9 3.3 slice-start.2
  643.1 1.3 slice-start.3
  644.4 1.5 copy-start.9
  649.0 1.4 copy-start.17
  650.4 1.4 copy-start.15
  802.1 9.2 %copy-start.19 = (f32[616,512]{1,0:T(8,128)S(1)}, f32[616,512]{1,0:T(8,128)}, u32[]{:S(2)}) copy-start(f32[616,512]{1,0:T(8,128)} %get-tuple-element.15) | copy-start | bytes 3784708
  802.1 10.4 %copy-start.1 = (bf16[616,512]{1,0:T(8,128)(2,1)S(1)}, bf16[616,512]{1,0:T(8,128)(2,1)}, u32[]{:S(2)}) copy-start(bf16[616,512]{1,0:T(8,128)(2,1)} %param.13) | copy-start | bytes 1892356
Sparse Core Ops, SparseCore 0:
  256.1 353.4 all-reduce.8
  612.2 189.8 all-reduce.10
